TPU v7x, 32 devices: a whole 2x2x4 slice. The times are simulated.
32 devices in a mesh: group: 8 (over z, x), fsdp: 4 (over y, core).
Axes of the slice: x: 2, y: 2, z: 4, core: 2. Of those that a mesh axis runs over, the one named last changes fastest.
Arguments:
- mol_qkv: bfloat16 [64, 128, 3, 4096], P('group', None, None, 'fsdp'), may hold values from -12 to 12
- pair_list: int32 [128, 3], replicated, may hold values from 0 to 7, as said below
- head_proj: bfloat16 [32, 128, 256], P('fsdp'), may hold values from -0.5 to 0.5
- head_out: float32 [32, 256], P('fsdp'), may hold values from -0.375 to 0.375
- labels: int32 [128], P('group'), may hold values 0 or 1
Outputs:
- mol_grad: bfloat16 [64, 128, 3, 4096], P('group', None, None, 'fsdp')
- pair_logits: float32 [128], P('group')
- mean_loss: float32 [], replicated
Inputs may be any that keep to these rules, and one draw needn't show every extreme that they name: `pair_list`: pair p belongs to owner p // 16; column 0 is the first molecule's index among the owner's 8 molecules, column 1 the group index that holds the second molecule, column 2 its index among that holder's 8 molecules; molecule m is held by group m // 8. `pair_list`: among one owner's pairs, at most 4 take their second molecule from any one holder, and those name at most 2 different molecules; every owner reaches both bounds.
All inputs are finite; a program needn't handle non-finite values. No bound on the sum of `labels` on one device may be relied on, other than what follows from the above.
Results may differ from a plain program's by a relative error of at most 0.0075.
Values may be sent and summed in bfloat16 or wider, within the bound.
A program may use at most 192 MiB of HBM per device.

v0:
```python
import jax
import jax.numpy as jnp
from jax import lax
from jax.sharding import PartitionSpec as P

loss_scale = 8192.0


def split_heads(rows_in, component, heads, head_dim):
    return rows_in[:, :, component].reshape(rows_in.shape[0], rows_in.shape[1], heads, head_dim)


def forward(query_rows, key_rows, value_rows, head_proj, head_out, inv_root, length):
    scores = (
        jnp.einsum("plhd,pmhd->phlm", query_rows, key_rows, preferred_element_type=jnp.float32)
        * inv_root
    )
    row_max = jnp.max(scores, axis=-1, keepdims=True)
    lifted = jnp.exp(scores - row_max)
    attn_weights = lifted / jnp.sum(lifted, axis=-1, keepdims=True)
    weights_bf = attn_weights.astype(jnp.bfloat16)
    context = jnp.einsum(
        "phlm,pmhd->plhd", weights_bf, value_rows, preferred_element_type=jnp.float32
    ).astype(jnp.bfloat16)
    hidden = jnp.einsum("plhd,hdr->plhr", context, head_proj, preferred_element_type=jnp.float32)
    partial_value = jnp.sum(jax.nn.silu(hidden) * head_out[None, None], axis=(1, 2, 3)) / length
    return (partial_value, (attn_weights, weights_bf, hidden))


def backward(
    query_rows, key_rows, value_rows, head_proj, head_out, saved, grad_out, inv_root, length
):
    attn_weights, weights_bf, hidden = saved
    sigmoid_h = jax.nn.sigmoid(hidden)
    silu_slope = sigmoid_h * (1.0 + hidden * (1.0 - sigmoid_h))
    dhidden = (grad_out[:, None, None, None] / length * head_out[None, None] * silu_slope).astype(
        jnp.bfloat16
    )
    dcontext = jnp.einsum(
        "plhr,hdr->plhd", dhidden, head_proj, preferred_element_type=jnp.float32
    ).astype(jnp.bfloat16)
    dvalues = jnp.einsum(
        "phlm,plhd->pmhd", weights_bf, dcontext, preferred_element_type=jnp.float32
    )
    dweights = jnp.einsum(
        "plhd,pmhd->phlm", dcontext, value_rows, preferred_element_type=jnp.float32
    )
    dscores = (
        attn_weights
        * (dweights - jnp.sum(dweights * attn_weights, axis=-1, keepdims=True))
        * inv_root
    ).astype(jnp.bfloat16)
    dqueries = jnp.einsum("phlm,pmhd->plhd", dscores, key_rows, preferred_element_type=jnp.float32)
    dkey_rows = jnp.einsum(
        "phlm,plhd->pmhd", dscores, query_rows, preferred_element_type=jnp.float32
    )
    return (dqueries, dkey_rows, dvalues)


def routing(blocks, mol_count, capacity, device):
    groups, per_owner, _ = blocks.shape
    holder = blocks[:, :, 1]
    member = blocks[:, :, 2]
    position = jnp.arange(per_owner, dtype=jnp.int32)
    mol_key = holder * mol_count + member
    matches = mol_key[:, :, None] == mol_key[:, None, :]
    earlier = matches & (position[None, None, :] < position[None, :, None])
    leading = jnp.logical_not(jnp.any(earlier, axis=2))
    leader = jnp.argmax(matches, axis=2)
    per_holder = (
        (holder[:, :, None] == jnp.arange(groups, dtype=jnp.int32)[None, None, :])
        & leading[:, :, None]
    ).astype(jnp.int32)
    rank_all = jnp.cumsum(per_holder, axis=1) - per_holder
    rank_in = jnp.take_along_axis(rank_all, holder[:, :, None], axis=2)[:, :, 0]
    slot_index = holder * capacity + rank_in
    return_slot = jnp.take_along_axis(slot_index, leader, axis=1)
    to_device = leading & (holder == device)
    picked = to_device[:, :, None] & (
        rank_in[:, :, None] == jnp.arange(capacity, dtype=jnp.int32)[None, None, :]
    )
    send_member = jnp.sum(picked.astype(jnp.int32) * member[:, :, None], axis=1)
    send_valid = jnp.any(picked, axis=1)
    return (return_slot, return_slot, send_member, send_valid)


def local(mol_qkv, pair_list, head_proj, head_out, labels):
    groups = lax.axis_size("group")
    device = lax.axis_index("group")
    mol_count, length, _, row_width = mol_qkv.shape
    heads_here, head_dim, inner_width = head_proj.shape
    total_pairs = pair_list.shape[0]
    per_owner = total_pairs // groups
    inv_root = head_dim ** (-0.5)
    blocks = pair_list.reshape(groups, per_owner, 3)
    capacity = per_owner // groups
    fetch_slot, return_slot, send_member, send_valid = routing(blocks, mol_count, capacity, device)
    slots_all = groups * capacity
    flat_member = send_member.reshape(slots_all)
    flat_valid = send_valid.reshape(slots_all)
    outgoing = jnp.take(mol_qkv, flat_member, axis=0)
    outgoing = jnp.where(flat_valid[:, None, None, None], outgoing, jnp.zeros_like(outgoing))
    incoming = lax.all_to_all(outgoing, "group", split_axis=0, concat_axis=0, tiled=True)
    my_pairs = lax.dynamic_index_in_dim(blocks, device, 0, keepdims=False)
    my_fetch = lax.dynamic_index_in_dim(fetch_slot, device, 0, keepdims=False)
    my_return = lax.dynamic_index_in_dim(return_slot, device, 0, keepdims=False)
    partner_rows = jnp.take(incoming, my_fetch, axis=0)
    own_rows = jnp.take(mol_qkv, my_pairs[:, 0], axis=0)
    qa, ka, va = [split_heads(own_rows, c, heads_here, head_dim) for c in range(3)]
    qb, kb, vb = [split_heads(partner_rows, c, heads_here, head_dim) for c in range(3)]
    part_ab, saved_ab = forward(qa, kb, vb, head_proj, head_out, inv_root, length)
    part_ba, saved_ba = forward(qb, ka, va, head_proj, head_out, inv_root, length)
    logits = lax.psum(part_ab + part_ba, "fsdp")
    targets = labels.astype(jnp.float32)
    loss_terms = jax.nn.softplus(logits) - targets * logits
    loss_sum = lax.psum(jnp.sum(loss_terms), "group")
    mean_loss = loss_sum / total_pairs
    grad_out = (jax.nn.sigmoid(logits) - targets) * loss_scale
    dq_a, dk_b, dv_b = backward(
        qa, kb, vb, head_proj, head_out, saved_ab, grad_out, inv_root, length
    )
    dq_b, dk_a, dv_a = backward(
        qb, ka, va, head_proj, head_out, saved_ba, grad_out, inv_root, length
    )
    grad_first = jnp.stack([dq_a, dk_a, dv_a], axis=2).reshape(per_owner, -1)
    grad_second = jnp.stack([dq_b, dk_b, dv_b], axis=2).reshape(per_owner, -1)
    own_pick = (my_pairs[:, 0][None, :] == jnp.arange(mol_count, dtype=jnp.int32)[:, None]).astype(
        jnp.float32
    )
    own_sum = jnp.dot(
        own_pick, grad_first, precision=lax.Precision.HIGHEST, preferred_element_type=jnp.float32
    )
    back_pick = (my_return[None, :] == jnp.arange(slots_all, dtype=jnp.int32)[:, None]).astype(
        jnp.float32
    )
    outgoing_grad = jnp.dot(
        back_pick, grad_second, precision=lax.Precision.HIGHEST, preferred_element_type=jnp.float32
    )
    outgoing_grad = outgoing_grad.astype(jnp.bfloat16).reshape(slots_all, length, 3, row_width)
    returned = lax.all_to_all(outgoing_grad, "group", split_axis=0, concat_axis=0, tiled=True)
    land_pick = (
        (flat_member[None, :] == jnp.arange(mol_count, dtype=jnp.int32)[:, None])
        & flat_valid[None, :]
    ).astype(jnp.bfloat16)
    partner_sum = jnp.dot(
        land_pick, returned.reshape(slots_all, -1), preferred_element_type=jnp.float32
    )
    mol_grad = (own_sum + partner_sum).astype(jnp.bfloat16).reshape(mol_qkv.shape)
    return (mol_grad, logits, mean_loss)


def solution(mesh):
    placed = (
        P("group", None, None, "fsdp"),
        P(),
        P("fsdp", None, None),
        P("fsdp", None),
        P("group"),
    )
    return jax.shard_map(
        local,
        mesh=mesh,
        in_specs=placed,
        out_specs=(P("group", None, None, "fsdp"), P("group"), P()),
        check_vma=False,
    )
```

profile of v0, /device:TPU:8, one launch (start us, length us, event | category | flops | bytes accessed | tf_op | source)
XLA Modules:
  0.0 1073.2 jit_solution(13335378748333062560)
XLA Ops:
  2.3 1.2 gather_fusion.1
  4.3 9.2 gather_fusion.3
  13.5 10.9 %select_select_fusion = bf16[16,128,3,1024]{3,1,2,0:T(8,128)(2,1)} fusion(bf16[16,128,3,1024]{3,1,2,0:T(8,128)(2,1)} %gather_fusion.3, pred[16]{0:T(512)(128)(4,1)S(1)} %get-tuple-element.46, pred[16]{0:T(512)(128)(4,1)S(1)} %broadcast_in_dim.42), kind=kLoop, calls=%fused_computation.43 | loop fusion | flops 12582912 | bytes 25165856 | tf_op jit(solution)/shard_map/jit(_where)/select_n | solution.py:102
  24.4 6.3 all-to-all-start
  31.7 1.0 gather_fusion.2
  32.8 9.2 gather_fusion.4
  42.0 6.5 broadcast_select_fusion
  48.6 4.8 fusion.170
  53.4 6.4 copy.119
  59.8 6.4 copy.128
  66.2 6.4 copy.126
  73.1 228.0 %all-to-all-done = bf16[16,128,3,1024]{3,1,2,0:T(8,128)(2,1)} async-done(((bf16[16,128,3,1024]{3,1,2,0:T(8,128)(2,1)}), bf16[16,128,3,1024]{3,1,2,0:T(8,128)(2,1)}, u32[]{:S(2)}, u32[]{:S(2)}) %all-to-all-start) | async-done | bytes 12582944 | tf_op jit(solution)/shard_map/all_to_all | solution.py:103
  301.1 11.1 %gather_fusion = bf16[16,128,3,1024]{3,1,2,0:T(8,128)(2,1)} fusion(bf16[16,128,3,1024]{3,1,2,0:T(8,128)(2,1)} %all-to-all-done, s32[1024]{0:T(1024)S(1)} %pad_clamp_fusion.1), kind=kCustom, calls=%fused_computation.2 | custom fusion | bytes 25165888 | tf_op jit(solution)/shard_map/jit(_take)/gather | solution.py:107
  312.2 6.5 broadcast_select_fusion.1
  318.8 4.9 fusion.169
  323.6 6.4 copy.122
  330.0 6.4 copy.127
  336.4 6.5 copy.118
  342.9 9.9 fusion.172
  352.8 9.9 fusion.171
  362.7 10.4 fusion.60
  373.1 19.0 %fusion.14 = (f32[16]{0:T(128)S(1)}, f32[16]{0:T(128)S(1)}, f32[8,16,128,256]{3,2,1,0:T(8,128)}) fusion(f32[8,256]{1,0:T(8,128)S(1)} %copy-done.6, f32[8,16,128,256]{3,2,1,0:T(8,128)} %fusion.60, bf16[8,128,256]{2,1,0:T(8,128)(2,1)S(1)} %copy-done, bf16[16,128,8,128]{1,3,2,0:T(8,128)(2,1)} %bitcast.196, f32[16,8,128,128]{2,3,1,0:T(8,128)} %get-tuple-element.42, ...), kind=kOutput, calls=%fused_computation.26 | convolution fusion | flops 1667235840 | bytes 46735488 | tf_op jit(solution)/shard_map/plhd,hdr->plhr/dot_general | solution.py:25
  392.1 7.1 psum.14
  399.9 9.9 convert_bitcast_fusion.1
  409.9 6.3 fusion.80
  416.2 9.7 fusion.110
  425.9 10.3 convert_bitcast_fusion
  436.2 2.0 copy-done.5
  438.2 6.3 fusion.76
  444.5 18.0 %fusion.101 = f32[16,128,1,8,128]{1,4,3,0,2:T(8,128)} fusion(bf16[16,128,8,128]{1,3,2,0:T(8,128)(2,1)} %bitcast.195, f32[16,8,128,128]{2,3,1,0:T(8,128)} %fusion.76, f32[16,8,128,128]{2,3,1,0:T(8,128)} %get-tuple-element.42, f32[16,8,128]{2,1,0:T(8,128)S(1)} %get-tuple-element.41), kind=kOutput, calls=%fused_computation.95 | convolution fusion | flops 551567488 | bytes 29425664 | tf_op jit(solution)/shard_map/phlm,pmhd->plhd/dot_general | solution.py:53
  462.5 18.1 %fusion.107 = f32[16,128,1,8,128]{1,4,3,0,2:T(8,128)} fusion(bf16[16,128,8,128]{1,3,2,0:T(8,128)(2,1)} %bitcast.193, f32[16,8,128,128]{2,3,1,0:T(8,128)} %fusion.80, f32[16,8,128,128]{2,3,1,0:T(8,128)} %get-tuple-element.44, f32[16,8,128]{2,1,0:T(8,128)S(1)} %get-tuple-element.43), kind=kOutput, calls=%fused_computation.97 | convolution fusion | flops 551567488 | bytes 29425664 | tf_op jit(solution)/shard_map/phlm,plhd->pmhd/dot_general | solution.py:54
  480.5 18.7 %pad_maximum_fusion.1 = f32[16,128,3,8,128]{1,4,3,0,2:T(8,128)} fusion(f32[16,128,1,8,128]{1,4,3,0,2:T(8,128)} %fusion.110, f32[16,128,1,8,128]{1,4,3,0,2:T(8,128)} %fusion.107, f32[16,128,1,8,128]{1,4,3,0,2:T(8,128)} %fusion.101), kind=kLoop, calls=%fused_computation.18 | loop fusion | flops 12582912 | bytes 50331648 | tf_op jit(solution)/shard_map/stack | solution.py:126
  499.2 24.7 %copy.147 = f32[16,128,3,8,128]{4,3,2,1,0:T(8,128)} copy(f32[16,128,3,8,128]{1,4,3,0,2:T(8,128)} %pad_maximum_fusion.1) | data formatting | bytes 50331648 | tf_op jit(solution)/shard_map/stack | solution.py:126
  523.9 34.5 %convolution_convert_fusion = bf16[16,393216]{1,0:T(8,128)(2,1)} fusion(f32[2,8,3072,128]{3,2,1,0:T(8,128)} %bitcast.189, s32[16]{0:T(128)S(1)} %copy-done.10), kind=kOutput, calls=%fused_computation.9 | convolution fusion | flops 1214251264 | bytes 37748800 | tf_op jit(solution)/shard_map/dot_general | solution.py:136
  558.4 30.0 %reshape.150 = bf16[16,128,3,1024]{3,2,1,0:T(4,128)(2,1)} reshape(bf16[16,393216]{1,0:T(8,128)(2,1)} %convolution_convert_fusion) | data formatting | bytes 25165824 | tf_op jit(solution)/shard_map/reshape | solution.py:139
  588.4 12.2 %copy.148 = bf16[16,128,3,1024]{3,1,2,0:T(8,128)(2,1)} copy(bf16[16,128,3,1024]{3,2,1,0:T(4,128)(2,1)} %reshape.150) | data formatting | bytes 25165824 | tf_op jit(solution)/shard_map/reshape | solution.py:139
  600.6 6.6 all-to-all-start.1
  607.9 281.0 %psum.15 = f32[]{:T(128)} all-reduce(f32[]{:T(128)} %get-tuple-element.39), channel_id=1, replica_groups=mesh['group'=8,'fsdp'=4] {'group'}, use_global_device_ids=true, to_apply=%region_15.17 | all-reduce | flops 1 | bytes 8 | tf_op jit(solution)/shard_map/psum | solution.py:116
  888.9 18.1 %fusion.98 = f32[16,128,1,8,128]{1,4,3,0,2:T(8,128)} fusion(bf16[16,128,8,128]{1,3,2,0:T(8,128)(2,1)} %bitcast.199, f32[16,8,128,128]{2,3,1,0:T(8,128)} %fusion.76, f32[16,8,128,128]{2,3,1,0:T(8,128)} %get-tuple-element.42, f32[16,8,128]{2,1,0:T(8,128)S(1)} %get-tuple-element.41), kind=kOutput, calls=%fused_computation.94 | convolution fusion | flops 551567488 | bytes 29425664 | tf_op jit(solution)/shard_map/phlm,plhd->pmhd/dot_general | solution.py:54
  907.0 17.9 %fusion.104 = f32[16,128,1,8,128]{1,4,3,0,2:T(8,128)} fusion(bf16[16,128,8,128]{1,3,2,0:T(8,128)(2,1)} %bitcast.201, f32[16,8,128,128]{2,3,1,0:T(8,128)} %fusion.80, f32[16,8,128,128]{2,3,1,0:T(8,128)} %get-tuple-element.44, f32[16,8,128]{2,1,0:T(8,128)S(1)} %get-tuple-element.43), kind=kOutput, calls=%fused_computation.96 | convolution fusion | flops 551567488 | bytes 29425664 | tf_op jit(solution)/shard_map/phlm,pmhd->plhd/dot_general | solution.py:53
  924.9 11.1 %fusion.113 = f32[16,128,1,8,128]{1,4,3,0,2:T(8,128)} fusion(bf16[16,128,8,128]{3,1,0,2:T(8,128)(2,1)} %copy-done.5, f32[16,8,128,128]{2,3,1,0:T(8,128)} %get-tuple-element.42, f32[16,8,128]{2,1,0:T(8,128)S(1)} %get-tuple-element.41), kind=kOutput, calls=%fused_computation.99 | convolution fusion | flops 541065216 | bytes 21037056 | tf_op jit(solution)/shard_map/phlm,plhd->pmhd/dot_general | solution.py:42
  936.0 15.5 %pad_maximum_fusion = f32[16,128,3,8,128]{1,4,3,0,2:T(8,128)} fusion(f32[16,128,1,8,128]{1,4,3,0,2:T(8,128)} %fusion.113, f32[16,128,1,8,128]{1,4,3,0,2:T(8,128)S(1)} %copy-done.4, f32[16,128,1,8,128]{1,4,3,0,2:T(8,128)} %fusion.104), kind=kLoop, calls=%fused_computation.17 | loop fusion | flops 12582912 | bytes 50331648 | tf_op jit(solution)/shard_map/stack | solution.py:125
  951.5 24.8 %copy.142 = f32[16,128,3,8,128]{4,3,2,1,0:T(8,128)} copy(f32[16,128,3,8,128]{1,4,3,0,2:T(8,128)} %pad_maximum_fusion) | data formatting | bytes 50331648 | tf_op jit(solution)/shard_map/stack | solution.py:125
  976.9 31.1 %fusion.7 = f32[8,393216]{1,0:T(8,128)} fusion(f32[2,8,3072,128]{3,2,1,0:T(8,128)} %bitcast.190, s32[16]{0:T(128)S(1)} %slice_bitcast_fusion.2), kind=kOutput, calls=%fused_computation.14 | convolution fusion | flops 603979904 | bytes 37748800 | tf_op jit(solution)/shard_map/dot_general | solution.py:130
  1008.0 18.7 %copy.149 = bf16[16,128,3,1024]{3,2,1,0:T(4,128)(2,1)} copy(bf16[16,128,3,1024]{3,1,2,0:T(8,128)(2,1)} %all-to-all-done.1) | data formatting | bytes 25165824 | tf_op jit(solution)/shard_map/all_to_all | solution.py:140
  1026.7 28.8 %reshape.151 = bf16[16,393216]{1,0:T(8,128)(2,1)} reshape(bf16[16,128,3,1024]{3,2,1,0:T(4,128)(2,1)} %copy.149) | data formatting | bytes 25165824 | tf_op jit(solution)/shard_map/reshape | solution.py:146
  1055.5 10.0 fusion.4
  1065.6 6.2 copy.150
  (71 shorter events, 5.5 us)
Async XLA Ops:
  0.6 362.1 %copy-start = (bf16[8,128,256]{2,1,0:T(8,128)(2,1)S(1)}, bf16[8,128,256]{2,1,0:T(8,128)(2,1)}, u32[]{:S(2)}) copy-start(bf16[8,128,256]{2,1,0:T(8,128)(2,1)} %param.9) | copy-start | bytes 1572868
  1.8 11.6 %copy-start.9 = (s32[1,16,3]{1,2,0:T(4,128)}, s32[1,16,3]{1,2,0:T(4,128)S(1)}, u32[]{:S(2)}) copy-start(s32[1,16,3]{1,2,0:T(4,128)S(1)} %copy.226) | copy-start | bytes 580
  4.1 9.4 copy-start.11
  4.3 9.2 copy-start.7
  24.4 276.7 %all-to-all-start = ((bf16[16,128,3,1024]{3,1,2,0:T(8,128)(2,1)}), bf16[16,128,3,1024]{3,1,2,0:T(8,128)(2,1)}, u32[]{:S(2)}, u32[]{:S(2)}) async-start(bf16[16,128,3,1024]{3,1,2,0:T(8,128)(2,1)} %select_select_fusion), calls=%async_computation | async-start | bytes 25165824 | tf_op jit(solution)/shard_map/all_to_all | solution.py:103
  362.7 10.4 copy-start.6
  373.1 26.1 %copy-start.13 = (s32[16]{0:T(128)S(1)}, s32[16]{0:T(128)}, u32[]{:S(2)}) copy-start(s32[16]{0:T(128)} %param.11) | copy-start | bytes 196
  399.2 10.6 copy-start.14
  399.9 9.9 copy-start.3
  425.9 12.3 %copy-start.2 = (bf16[16,128,1,1024]{1,3,0,2:T(8,128)(2,1)S(1)}, bf16[16,128,1,1024]{1,3,0,2:T(8,128)(2,1)}, u32[]{:S(2)}) copy-start(bf16[16,128,1,1024]{1,3,0,2:T(8,128)(2,1)} %copy.126) | copy-start | bytes 12582916
  436.2 2.0 copy-start.5
  499.2 24.7 %copy-start.10 = (s32[16]{0:T(128)S(1)}, s32[16]{0:T(128)}, u32[]{:S(2)}) copy-start(s32[16]{0:T(128)} %get-tuple-element.26) | copy-start | bytes 196
  600.6 407.3 %all-to-all-start.1 = ((bf16[16,128,3,1024]{3,1,2,0:T(8,128)(2,1)}), bf16[16,128,3,1024]{3,1,2,0:T(8,128)(2,1)}, u32[]{:S(2)}, u32[]{:S(2)}) async-start(bf16[16,128,3,1024]{3,1,2,0:T(8,128)(2,1)} %copy.148), calls=%async_computation.1 | async-start | bytes 25165824 | tf_op jit(solution)/shard_map/all_to_all | solution.py:140
  924.9 11.1 %copy-start.4 = (f32[16,128,1,8,128]{1,4,3,0,2:T(8,128)S(1)}, f32[16,128,1,8,128]{1,4,3,0,2:T(8,128)}, u32[]{:S(2)}) copy-start(f32[16,128,1,8,128]{1,4,3,0,2:T(8,128)} %fusion.98) | copy-start | bytes 25165828
  1026.7 28.8 %copy-start.8 = (s32[16]{0:T(128)S(1)}, s32[16]{0:T(128)}, u32[]{:S(2)}) copy-start(s32[16]{0:T(128)} %copy-done.7) | copy-start | bytes 196
  1026.7 28.8 %copy-start.12 = (pred[16]{0:T(512)(128)(4,1)S(1)}, pred[16]{0:T(512)(128)(4,1)}, u32[]{:S(2)}) copy-start(pred[16]{0:T(512)(128)(4,1)} %copy-done.11) | copy-start | bytes 52
  1055.5 16.3 %copy-start.1 = (bf16[8,128,256]{2,1,0:T(8,128)(2,1)S(1)}, bf16[8,128,256]{2,1,0:T(8,128)(2,1)}, u32[]{:S(2)}) copy-start(bf16[8,128,256]{2,1,0:T(8,128)(2,1)} %param.9) | copy-start | bytes 1572868
where the time goes:
time: 1080 us; the launch traced here: 1070 us
  blocking collectives  288 us (27%)
  matrix products  250 us (23%)
  local copies, waits for them, and re-layouts  230 us (21%)
  waiting for transfers between devices  228 us (21%)
  other arithmetic  61.2 us (6%)
  starting transfers between devices  12.8 us (1%)
    psum x1, blocking collectives, local(): loss_sum = lax.psum(jnp.sum(loss_terms), 'group')  281 us
    all_to_all x1, waiting for transfers between devices, local(): lax.all_to_all(outgoing, 'group', split_axis=0, concat_axis=0, tiled=True)  228 us
    slice x8, local copies, waits for them, and re-layouts, split_heads(): rows_in[:, :, component]  48.1 us
    reshape x2, local copies, waits for them, and re-layouts, local(): outgoing_grad.astype(jnp.bfloat16).reshape(slots_all, length, 3, row_width)  42.3 us
    dot_general x2, matrix products, backward(): jnp.einsum('phlm,plhd->pmhd', dscores, query_rows, preferred_element_type...  36.2 us
    dot_general x2, matrix products, backward(): jnp.einsum('phlm,pmhd->plhd', dscores, key_rows, preferred_element_type=j...  35.9 us
    dot_general x1, matrix products, local(): jnp.dot(back_pick, grad_second, precision=lax.Precision.HIGHEST, preferre...  34.5 us
    dot_general x1, matrix products, local(): jnp.dot(own_pick, grad_first, precision=lax.Precision.HIGHEST, preferred_...  31.1 us
  transfers between devices with their start and end apart: 2, of which 1 were waited for; matrix products, arithmetic and copies ran while one was open for 15% of the time, Pallas kernels for 0%

commit v1 on v0

--- a/solution.py
+++ b/solution.py
@@ -4,6 +4,18 @@
 from jax.sharding import PartitionSpec as P
 
 loss_scale = 8192.0
+
+
+def split_up(x, dim, size):
+    shape = x.shape
+    parts = x.reshape(*shape[:dim], size, shape[dim] // size, *shape[dim + 1 :])
+    return jnp.moveaxis(parts, dim, 0)
+
+
+def in_order(pieces, dim):
+    dims = list(pieces.shape[1:])
+    dims[dim] *= pieces.shape[0]
+    return jnp.moveaxis(pieces, 0, dim).reshape(dims)
 
 
 def split_heads(rows_in, component, heads, head_dim):
@@ -100,7 +112,14 @@
     flat_valid = send_valid.reshape(slots_all)
     outgoing = jnp.take(mol_qkv, flat_member, axis=0)
     outgoing = jnp.where(flat_valid[:, None, None, None], outgoing, jnp.zeros_like(outgoing))
-    incoming = lax.all_to_all(outgoing, "group", split_axis=0, concat_axis=0, tiled=True)
+    size, index = (lax.axis_size("group"), lax.axis_index("group"))
+    tiles = split_up(outgoing, 0, size)
+    finished = [tiles[index]]
+    for turn in range(1, size):
+        sent = tiles[(index + turn) % size]
+        finished.append(lax.ppermute(sent, "group", [(i, (i + turn) % size) for i in range(size)]))
+    tiles = jnp.stack(finished)[(index - jnp.arange(size)) % size]
+    incoming = in_order(tiles, 0)
     my_pairs = lax.dynamic_index_in_dim(blocks, device, 0, keepdims=False)
     my_fetch = lax.dynamic_index_in_dim(fetch_slot, device, 0, keepdims=False)
     my_return = lax.dynamic_index_in_dim(return_slot, device, 0, keepdims=False)

time: 1080 us -> 1140 us (1.056)
  local copies, waits for them, and re-layouts: 230 us -> 263 us
  waiting for transfers between devices: 228 us -> 244 us
    ppermute x0 -> x7, waiting for transfers between devices: none -> 244 us  [local(): lax.ppermute(sent, 'group', [(i, (i + turn) % size) for i in range(size)])]
    all_to_all x1 -> x0, waiting for transfers between devices: 228 us -> none  [local(): lax.all_to_all(outgoing, 'group', split_axis=0, concat_axis=0, tiled=True)]
    unnamed x34 -> x42, local copies, waits for them, and re-layouts: 8.36 us -> 24 us
    dot_general x2, matrix products: 29.4 us -> 41.1 us  [forward(): jnp.einsum('plhd,hdr->plhr', context, head_proj, preferred_element_type=j...]
  transfers between devices with their start and end apart: 2 -> 8, of which waited for: 1 -> 3; matrix products, arithmetic and copies ran while one was open for 15% -> 16% of each run, Pallas kernels for 0% -> 0%
where the time goes in v1:
time: 1140 us; the launch traced here: 1130 us
  blocking collectives  286 us (25%)
  local copies, waits for them, and re-layouts  263 us (23%)
  matrix products  259 us (23%)
  waiting for transfers between devices  244 us (21%)
  other arithmetic  57.1 us (5%)
  starting transfers between devices  15.8 us (1%)
    psum x1, blocking collectives, local(): loss_sum = lax.psum(jnp.sum(loss_terms), 'group')  281 us
    ppermute x7, waiting for transfers between devices, local(): lax.ppermute(sent, 'group', [(i, (i + turn) % size) for i in range(size)])  244 us
    slice x8, local copies, waits for them, and re-layouts, split_heads(): rows_in[:, :, component]  48 us
    reshape x2, local copies, waits for them, and re-layouts, local(): outgoing_grad.astype(jnp.bfloat16).reshape(slots_all, length, 3, row_width)  42.1 us
    dot_general x2, matrix products, forward(): jnp.einsum('plhd,hdr->plhr', context, head_proj, preferred_element_type=j...  41.1 us
    dot_general x2, matrix products, backward(): jnp.einsum('phlm,plhd->pmhd', dscores, query_rows, preferred_element_type...  35.9 us
    dot_general x2, matrix products, backward(): jnp.einsum('phlm,pmhd->plhd', dscores, key_rows, preferred_element_type=j...  35.8 us
    dot_general x1, matrix products, local(): jnp.dot(back_pick, grad_second, precision=lax.Precision.HIGHEST, preferre...  34.7 us
  transfers between devices with their start and end apart: 8, of which 3 were waited for; matrix products, arithmetic and copies ran while one was open for 16% of the time, Pallas kernels for 0%

profile of v1, /device:TPU:8, one launch (start us, length us, event | category | flops | bytes accessed | tf_op | source)
XLA Modules:
  0.0 1127.0 jit_solution(12265406891173305766)
XLA Ops:
  5.9 9.2 gather_fusion.4
  15.1 6.7 select_select_fusion
  21.8 4.7 dynamic-slice_bitcast_fusion
  34.4 9.2 gather_fusion.5
  43.7 6.5 broadcast_select_fusion
  50.2 4.8 fusion.172
  56.3 210.0 %collective-permute-done.1 = bf16[2,128,3,1024]{3,1,2,0:T(8,128)(2,1)} collective-permute-done((bf16[2,128,3,1024]{3,1,2,0:T(8,128)(2,1)}, bf16[2,128,3,1024]{3,1,2,0:T(8,128)(2,1)}, u32[]{:S(2)}, u32[]{:S(2)}) %collective-permute-start.1) | collective-permute-done | bytes 1572896 | tf_op jit(solution)/shard_map/ppermute | solution.py:120
  266.8 6.4 copy.119
  273.2 6.4 copy.128
  279.6 6.4 copy.126
  298.4 5.8 collective-permute-done.5
  307.0 27.7 %collective-permute-done.6 = bf16[2,128,3,1024]{3,1,2,0:T(8,128)(2,1)S(1)} collective-permute-done((bf16[2,128,3,1024]{3,1,2,0:T(8,128)(2,1)}, bf16[2,128,3,1024]{3,1,2,0:T(8,128)(2,1)S(1)}, u32[]{:S(2)}, u32[]{:S(2)}) %collective-permute-start.6) | collective-permute-done | bytes 1572896 | tf_op jit(solution)/shard_map/ppermute | solution.py:120
  336.0 11.3 %gather_fusion = bf16[8,2,128,3,1024]{4,2,3,1,0:T(8,128)(2,1)} fusion(bf16[8,2,128,3,1024]{4,2,3,1,0:T(8,128)(2,1)} %bitcast_dynamic-update-slice_fusion, s32[1024]{0:T(1024)S(1)} %pad_clamp_fusion.2), kind=kCustom, calls=%fused_computation.2 | custom fusion | bytes 25165856 | tf_op jit(solution)/shard_map/gather | solution.py:121
  347.3 11.1 gather_fusion.1
  358.4 6.5 broadcast_select_fusion.1
  364.9 4.8 fusion.171
  369.7 6.4 copy.122
  376.1 6.4 copy.127
  382.5 6.4 copy.118
  388.9 10.0 fusion.173
  398.8 9.9 fusion.174
  408.7 10.4 fusion.60
  419.1 30.8 %fusion.14 = (f32[16]{0:T(128)S(1)}, f32[16]{0:T(128)S(1)}, f32[8,16,128,256]{3,2,1,0:T(8,128)}) fusion(f32[8,256]{1,0:T(8,128)S(1)} %copy-done.7, f32[8,16,128,256]{3,2,1,0:T(8,128)} %fusion.60, bf16[8,128,256]{2,1,0:T(8,128)(2,1)S(1)} %copy-done, bf16[16,128,8,128]{1,3,2,0:T(8,128)(2,1)} %bitcast.230, f32[16,8,128,128]{2,3,1,0:T(8,128)} %get-tuple-element.50, ...), kind=kOutput, calls=%fused_computation.27 | convolution fusion | flops 1667235840 | bytes 46735488 | tf_op jit(solution)/shard_map/plhd,hdr->plhr/dot_general | solution.py:37
  449.8 5.9 psum.14
  456.5 9.9 convert_bitcast_fusion.1
  466.4 6.4 fusion.80
  472.8 6.3 fusion.110
  479.1 10.1 convert_bitcast_fusion
  491.1 6.4 fusion.76
  497.5 17.9 %fusion.101 = f32[16,128,1,8,128]{1,4,3,0,2:T(8,128)} fusion(bf16[16,128,8,128]{1,3,2,0:T(8,128)(2,1)} %bitcast.229, f32[16,8,128,128]{2,3,1,0:T(8,128)} %fusion.76, f32[16,8,128,128]{2,3,1,0:T(8,128)} %get-tuple-element.50, f32[16,8,128]{2,1,0:T(8,128)S(1)} %get-tuple-element.49), kind=kOutput, calls=%fused_computation.96 | convolution fusion | flops 551567488 | bytes 29425664 | tf_op jit(solution)/shard_map/phlm,pmhd->plhd/dot_general | solution.py:65
  515.4 17.9 %fusion.107 = f32[16,128,1,8,128]{1,4,3,0,2:T(8,128)} fusion(bf16[16,128,8,128]{1,3,2,0:T(8,128)(2,1)} %bitcast.227, f32[16,8,128,128]{2,3,1,0:T(8,128)} %fusion.80, f32[16,8,128,128]{2,3,1,0:T(8,128)} %get-tuple-element.52, f32[16,8,128]{2,1,0:T(8,128)S(1)} %get-tuple-element.51), kind=kOutput, calls=%fused_computation.98 | convolution fusion | flops 551567488 | bytes 29425664 | tf_op jit(solution)/shard_map/phlm,plhd->pmhd/dot_general | solution.py:66
  533.3 18.7 %pad_maximum_fusion.1 = f32[16,128,3,8,128]{1,4,3,0,2:T(8,128)} fusion(f32[16,128,1,8,128]{1,4,3,0,2:T(8,128)} %fusion.110, f32[16,128,1,8,128]{1,4,3,0,2:T(8,128)} %fusion.107, f32[16,128,1,8,128]{1,4,3,0,2:T(8,128)} %fusion.101), kind=kLoop, calls=%fused_computation.19 | loop fusion | flops 12582912 | bytes 50331648 | tf_op jit(solution)/shard_map/stack | solution.py:145
  552.0 24.7 %copy.147 = f32[16,128,3,8,128]{4,3,2,1,0:T(8,128)} copy(f32[16,128,3,8,128]{1,4,3,0,2:T(8,128)} %pad_maximum_fusion.1) | data formatting | bytes 50331648 | tf_op jit(solution)/shard_map/stack | solution.py:145
  576.7 34.7 %convolution_convert_fusion = bf16[16,393216]{1,0:T(8,128)(2,1)} fusion(f32[2,8,3072,128]{3,2,1,0:T(8,128)} %bitcast.221, s32[16]{0:T(128)S(1)} %copy-done.8), kind=kOutput, calls=%fused_computation.10 | convolution fusion | flops 1214251264 | bytes 37748800 | tf_op jit(solution)/shard_map/dot_general | solution.py:155
  611.4 29.9 %reshape.207 = bf16[16,128,3,1024]{3,2,1,0:T(4,128)(2,1)} reshape(bf16[16,393216]{1,0:T(8,128)(2,1)} %convolution_convert_fusion) | data formatting | bytes 25165824 | tf_op jit(solution)/shard_map/reshape | solution.py:158
  641.3 12.2 %copy.148 = bf16[16,128,3,1024]{3,1,2,0:T(8,128)(2,1)} copy(bf16[16,128,3,1024]{3,2,1,0:T(4,128)(2,1)} %reshape.207) | data formatting | bytes 25165824 | tf_op jit(solution)/shard_map/reshape | solution.py:158
  653.5 7.9 all-to-all-start
  662.1 280.5 %psum.15 = f32[]{:T(128)} all-reduce(f32[]{:T(128)} %get-tuple-element.47), channel_id=1, replica_groups=mesh['group'=8,'fsdp'=4] {'group'}, use_global_device_ids=true, to_apply=%region_15.17 | all-reduce | flops 1 | bytes 8 | tf_op jit(solution)/shard_map/psum | solution.py:135
  942.6 18.0 %fusion.98 = f32[16,128,1,8,128]{1,4,3,0,2:T(8,128)} fusion(bf16[16,128,8,128]{1,3,2,0:T(8,128)(2,1)} %bitcast.233, f32[16,8,128,128]{2,3,1,0:T(8,128)} %fusion.76, f32[16,8,128,128]{2,3,1,0:T(8,128)} %get-tuple-element.50, f32[16,8,128]{2,1,0:T(8,128)S(1)} %get-tuple-element.49), kind=kOutput, calls=%fused_computation.95 | convolution fusion | flops 551567488 | bytes 29425664 | tf_op jit(solution)/shard_map/phlm,plhd->pmhd/dot_general | solution.py:66
  960.6 17.9 %fusion.104 = f32[16,128,1,8,128]{1,4,3,0,2:T(8,128)} fusion(bf16[16,128,8,128]{1,3,2,0:T(8,128)(2,1)} %bitcast.235, f32[16,8,128,128]{2,3,1,0:T(8,128)} %fusion.80, f32[16,8,128,128]{2,3,1,0:T(8,128)} %get-tuple-element.52, f32[16,8,128]{2,1,0:T(8,128)S(1)} %get-tuple-element.51), kind=kOutput, calls=%fused_computation.97 | convolution fusion | flops 551567488 | bytes 29425664 | tf_op jit(solution)/shard_map/phlm,pmhd->plhd/dot_general | solution.py:65
  978.5 11.1 fusion.113
  989.5 15.5 %pad_maximum_fusion = f32[16,128,3,8,128]{1,4,3,0,2:T(8,128)} fusion(f32[16,128,1,8,128]{1,4,3,0,2:T(8,128)} %fusion.113, f32[16,128,1,8,128]{1,4,3,0,2:T(8,128)S(1)} %copy-done.5, f32[16,128,1,8,128]{1,4,3,0,2:T(8,128)} %fusion.104), kind=kLoop, calls=%fused_computation.18 | loop fusion | flops 12582912 | bytes 50331648 | tf_op jit(solution)/shard_map/stack | solution.py:144
  1005.0 24.7 %copy.142 = f32[16,128,3,8,128]{4,3,2,1,0:T(8,128)} copy(f32[16,128,3,8,128]{1,4,3,0,2:T(8,128)} %pad_maximum_fusion) | data formatting | bytes 50331648 | tf_op jit(solution)/shard_map/stack | solution.py:144
  1030.3 31.2 %fusion.7 = f32[8,393216]{1,0:T(8,128)} fusion(f32[2,8,3072,128]{3,2,1,0:T(8,128)} %bitcast.222, s32[16]{0:T(128)S(1)} %slice_bitcast_fusion.2), kind=kOutput, calls=%fused_computation.15 | convolution fusion | flops 603979904 | bytes 37748800 | tf_op jit(solution)/shard_map/dot_general | solution.py:149
  1061.6 18.7 %copy.149 = bf16[16,128,3,1024]{3,2,1,0:T(4,128)(2,1)} copy(bf16[16,128,3,1024]{3,1,2,0:T(8,128)(2,1)} %all-to-all-done) | data formatting | bytes 25165824 | tf_op jit(solution)/shard_map/all_to_all | solution.py:159
  1080.3 29.1 %reshape.208 = bf16[16,393216]{1,0:T(8,128)(2,1)} reshape(bf16[16,128,3,1024]{3,2,1,0:T(4,128)(2,1)} %copy.149) | data formatting | bytes 25165824 | tf_op jit(solution)/shard_map/reshape | solution.py:165
  1109.4 10.0 fusion.4
  1119.5 6.2 copy.150
  (96 shorter events, 34.6 us)
Async XLA Ops:
  0.6 408.1 %copy-start = (bf16[8,128,256]{2,1,0:T(8,128)(2,1)S(1)}, bf16[8,128,256]{2,1,0:T(8,128)(2,1)}, u32[]{:S(2)}) copy-start(bf16[8,128,256]{2,1,0:T(8,128)(2,1)} %param.9) | copy-start | bytes 1572868
  5.1 0.6 copy-start.12
  5.9 9.2 copy-start.10
  26.5 270.5 %collective-permute-start.4 = (bf16[2,128,3,1024]{3,1,2,0:T(8,128)(2,1)}, bf16[2,128,3,1024]{3,1,2,0:T(8,128)(2,1)S(1)}, u32[]{:S(2)}, u32[]{:S(2)}) collective-permute-start(bf16[2,128,3,1024]{3,1,2,0:T(8,128)(2,1)} %get-tuple-element.37), channel_id=1, source_target_pairs={{0,20},{4,24},{8,28},{12,0},{16,4},{20,8},{24,12},{28,16},{1,21},{... | collective-permute-start | bytes 4718600 | tf_op jit(solution)/shard_map/ppermute | solution.py:120
  30.0 264.3 %collective-permute-start.3 = (bf16[2,128,3,1024]{3,1,2,0:T(8,128)(2,1)}, bf16[2,128,3,1024]{3,1,2,0:T(8,128)(2,1)}, u32[]{:S(2)}, u32[]{:S(2)}) collective-permute-start(bf16[2,128,3,1024]{3,1,2,0:T(8,128)(2,1)} %get-tuple-element.38), channel_id=1, source_target_pairs={{0,16},{4,20},{8,24},{12,28},{16,0},{20,4},{24,8},{28,12},{1,17},{... | collective-permute-start | bytes 4718600 | tf_op jit(solution)/shard_map/ppermute | solution.py:120
  30.5 261.0 %collective-permute-start.2 = (bf16[2,128,3,1024]{3,1,2,0:T(8,128)(2,1)}, bf16[2,128,3,1024]{3,1,2,0:T(8,128)(2,1)}, u32[]{:S(2)}, u32[]{:S(2)}) collective-permute-start(bf16[2,128,3,1024]{3,1,2,0:T(8,128)(2,1)} %get-tuple-element.39), channel_id=1, source_target_pairs={{0,12},{4,16},{8,20},{12,24},{16,28},{20,0},{24,4},{28,8},{1,13},{... | collective-permute-start | bytes 4718600 | tf_op jit(solution)/shard_map/ppermute | solution.py:120
  33.0 233.2 %collective-permute-start.1 = (bf16[2,128,3,1024]{3,1,2,0:T(8,128)(2,1)}, bf16[2,128,3,1024]{3,1,2,0:T(8,128)(2,1)}, u32[]{:S(2)}, u32[]{:S(2)}) collective-permute-start(bf16[2,128,3,1024]{3,1,2,0:T(8,128)(2,1)} %get-tuple-element.40), channel_id=1, source_target_pairs={{0,8},{4,12},{8,16},{12,20},{16,24},{20,28},{24,0},{28,4},{1,9},{5... | collective-permute-start | bytes 4718600 | tf_op jit(solution)/shard_map/ppermute | solution.py:120
  33.0 252.9 %collective-permute-start = (bf16[2,128,3,1024]{3,1,2,0:T(8,128)(2,1)}, bf16[2,128,3,1024]{3,1,2,0:T(8,128)(2,1)}, u32[]{:S(2)}, u32[]{:S(2)}) collective-permute-start(bf16[2,128,3,1024]{3,1,2,0:T(8,128)(2,1)} %get-tuple-element.41), channel_id=1, source_target_pairs={{0,4},{4,8},{8,12},{12,16},{16,20},{20,24},{24,28},{28,0},{1,5},{5... | collective-permute-start | bytes 4718600 | tf_op jit(solution)/shard_map/ppermute | solution.py:120
  34.4 9.2 copy-start.9
  266.3 38.0 %collective-permute-start.5 = (bf16[2,128,3,1024]{3,1,2,0:T(8,128)(2,1)}, bf16[2,128,3,1024]{3,1,2,0:T(8,128)(2,1)}, u32[]{:S(2)}, u32[]{:S(2)}) collective-permute-start(bf16[2,128,3,1024]{3,1,2,0:T(8,128)(2,1)} %get-tuple-element.36), channel_id=1, source_target_pairs={{0,24},{4,28},{8,0},{12,4},{16,8},{20,12},{24,16},{28,20},{1,25},{... | collective-permute-start | bytes 4718600 | tf_op jit(solution)/shard_map/ppermute | solution.py:120
  286.0 48.8 %collective-permute-start.6 = (bf16[2,128,3,1024]{3,1,2,0:T(8,128)(2,1)}, bf16[2,128,3,1024]{3,1,2,0:T(8,128)(2,1)S(1)}, u32[]{:S(2)}, u32[]{:S(2)}) collective-permute-start(bf16[2,128,3,1024]{3,1,2,0:T(8,128)(2,1)} %get-tuple-element.35), channel_id=1, source_target_pairs={{0,28},{4,0},{8,4},{12,8},{16,12},{20,16},{24,20},{28,24},{1,29},{... | collective-permute-start | bytes 4718600 | tf_op jit(solution)/shard_map/ppermute | solution.py:120
  408.7 10.4 copy-start.7
  419.1 36.7 %copy-start.14 = (s32[16]{0:T(128)S(1)}, s32[16]{0:T(128)}, u32[]{:S(2)}) copy-start(s32[16]{0:T(128)} %param.11) | copy-start | bytes 196
  455.7 0.7 copy-start.15
  456.5 9.9 copy-start.3
  466.4 6.4 copy-start.4
  479.1 12.0 %copy-start.2 = (bf16[16,128,1,1024]{1,3,0,2:T(8,128)(2,1)S(1)}, bf16[16,128,1,1024]{1,3,0,2:T(8,128)(2,1)}, u32[]{:S(2)}) copy-start(bf16[16,128,1,1024]{1,3,0,2:T(8,128)(2,1)} %copy.126) | copy-start | bytes 12582916
  489.2 1.9 copy-start.6
  552.0 24.7 %copy-start.8 = (s32[16]{0:T(128)S(1)}, s32[16]{0:T(128)}, u32[]{:S(2)}) copy-start(s32[16]{0:T(128)} %get-tuple-element.26) | copy-start | bytes 196
  653.5 408.0 %all-to-all-start = ((bf16[16,128,3,1024]{3,1,2,0:T(8,128)(2,1)}), bf16[16,128,3,1024]{3,1,2,0:T(8,128)(2,1)}, u32[]{:S(2)}, u32[]{:S(2)}) async-start(bf16[16,128,3,1024]{3,1,2,0:T(8,128)(2,1)} %copy.148), calls=%async_computation | async-start | bytes 25165824 | tf_op jit(solution)/shard_map/all_to_all | solution.py:159
  978.5 11.1 copy-start.5
  1080.3 29.1 %copy-start.11 = (pred[16]{0:T(512)(128)(4,1)S(1)}, pred[16]{0:T(512)(128)(4,1)}, u32[]{:S(2)}) copy-start(pred[16]{0:T(512)(128)(4,1)} %copy-done.10) | copy-start | bytes 52
  1080.3 29.1 %copy-start.13 = (s32[16]{0:T(128)S(1)}, s32[16]{0:T(128)}, u32[]{:S(2)}) copy-start(s32[16]{0:T(128)} %copy-done.12) | copy-start | bytes 196
  1109.4 16.3 %copy-start.1 = (bf16[8,128,256]{2,1,0:T(8,128)(2,1)S(1)}, bf16[8,128,256]{2,1,0:T(8,128)(2,1)}, u32[]{:S(2)}) copy-start(bf16[8,128,256]{2,1,0:T(8,128)(2,1)} %param.9) | copy-start | bytes 1572868
